TPU v7x, 32 devices: a whole 2x2x4 slice. The times are simulated.
32 devices in a mesh: section: 16 (over z, y, x), tensor: 2 (over core).
Axes of the slice: x: 2, y: 2, z: 4, core: 2. Of those that a mesh axis runs over, the one named last changes fastest.
Arguments:
- embedded: bfloat16 [256, 4096], P(None, 'tensor'), may hold values from -6 to 6
- outbox: bfloat16 [16, 256, 4096], P('section', None, 'tensor'), may hold values from -6 to 6
- loss_grad: bfloat16 [256, 4096], P(None, 'tensor'), may hold values from -6 to 6
- grad_outbox: bfloat16 [16, 256, 4096], P('section', None, 'tensor'), may hold values from -6 to 6
- stash_held: bfloat16 [16, 256, 4096], P('section', None, 'tensor'), may hold values from -6 to 6
- norm_gain: bfloat16 [16, 4096], P('section', 'tensor'), may hold values from 0.099609375 to 1.8984375
- w_query: bfloat16 [16, 4096, 1024], P('section', None, 'tensor'), may hold values from -4 to 4
- w_keyval: bfloat16 [16, 4096, 512], P('section', None, 'tensor'), may hold values from -1 to 1
- w_out: bfloat16 [16, 1024, 4096], P('section', 'tensor'), may hold values from -0.25 to 0.25
Outputs:
- section_out: bfloat16 [16, 256, 4096], P('section', None, 'tensor')
- evicted: bfloat16 [16, 256, 4096], P('section', None, 'tensor')
- input_grad: bfloat16 [16, 256, 4096], P('section', None, 'tensor')
All inputs are finite; a program needn't handle non-finite values.
Results may differ from a plain program's by a relative error of at most 0.013.
Values may be sent and summed in bfloat16 or wider, within the bound.
No kernel may reach another device: no remote copies, remote signals or barrier semaphores. Data moves between devices by JAX's collectives and lax.ppermute only.
A program may use at most 64 MiB of HBM per device.

v0:
```python
import functools

import jax
import jax.numpy as jnp
from jax import lax
from jax.experimental import pallas as pl
from jax.experimental.pallas import tpu as pltpu
from jax.sharding import PartitionSpec as P


HEAD = 128
EPS = 1e-05
SCALE = HEAD ** (-0.5)
F32 = jnp.float32
BF16 = jnp.bfloat16


def rotate(value, axis, k):
    count = lax.axis_size(axis)
    return lax.ppermute(value, axis, [(i, (i - k) % count) for i in range(count)])


def gathered(value, axis):
    return [value] + [rotate(value, axis, k) for k in range(1, lax.axis_size(axis))]


def reduced(parts, axis):
    total = parts[0].astype(F32)
    for k in range(1, len(parts)):
        total = total + rotate(parts[k], axis, -k).astype(F32)
    return total


def nt(a, b):
    return lax.dot_general(a, b, (((1,), (1,)), ((), ())), preferred_element_type=F32)


def tn(a, b):
    return lax.dot_general(a, b, (((0,), (0,)), ((), ())), preferred_element_type=F32)


def nn(a, b):
    return jnp.dot(a, b, preferred_element_type=F32)


def vmem_spec():
    return pl.BlockSpec(memory_space=pltpu.VMEM)


def any_spec():
    return pl.BlockSpec(memory_space=pl.ANY)


def load_rows(col, count, hbm, buf, sem):
    width = hbm.shape[0] // count
    copies = []
    for k in range(count):
        block = lax.rem(col + k, count)
        copies.append(
            pltpu.make_async_copy(
                hbm.at[pl.ds(pl.multiple_of(block * width, width), width), :],
                buf.at[pl.ds(k * width, width), :],
                sem.at[k],
            )
        )
    for copy in copies:
        copy.start()
    return copies


def load_columns(col, count, hbm, buf, sem):
    width = hbm.shape[1] // count
    copies = []
    for k in range(count):
        block = lax.rem(col + k, count)
        copies.append(
            pltpu.make_async_copy(
                hbm.at[:, pl.ds(pl.multiple_of(block * width, width), width)],
                buf.at[k],
                sem.at[k],
            )
        )
    for copy in copies:
        copy.start()
    return copies


def normalize(xs, gains, normed):
    width = xs[0].shape[1]
    total = None
    for x in xs:
        xf = x[...].astype(F32)
        part = jnp.sum(xf * xf, axis=-1, keepdims=True)
        total = part if total is None else total + part
    inv = lax.rsqrt(total / (width * len(xs)) + EPS)
    for k, x in enumerate(xs):
        xf = x[...].astype(F32)
        normed[:, k * width : (k + 1) * width] = (xf * inv * gains[k][...].astype(F32)).astype(BF16)
    return inv


def causal_mask(seq):
    rows = lax.broadcasted_iota(jnp.int32, (seq, seq), 0)
    cols = lax.broadcasted_iota(jnp.int32, (seq, seq), 1)
    return rows >= cols


def softmax(query, keys, mask):
    scores = jnp.where(mask, nt(query, keys) * SCALE, -1e30)
    top = jnp.max(scores, axis=-1, keepdims=True)
    weights = jnp.exp(scores - top)
    return weights / jnp.sum(weights, axis=-1, keepdims=True)


def forward_kernel(count, heads, *refs):
    xs, refs = refs[:count], refs[count:]
    gains, refs = refs[:count], refs[count:]
    wq_hbm, wkv_hbm, wo_hbm, refs = *refs[:3], refs[3:]
    outs, refs = refs[:count], refs[count:]
    normed, wq, wkv, wo, attn, sems = refs
    col = lax.axis_index("tensor")
    first = load_rows(col, count, wq_hbm, wq, sems.at[0])
    first += load_rows(col, count, wkv_hbm, wkv, sems.at[1])
    last = load_columns(col, count, wo_hbm, wo, sems.at[2])
    normalize(xs, gains, normed)
    for copy in first:
        copy.wait()
    keyval = nn(normed[...], wkv[...]).astype(BF16)
    query = nn(normed[...], wq[...]).astype(BF16)
    keys, values = keyval[:, :HEAD], keyval[:, HEAD:]
    mask = causal_mask(query.shape[0])
    for h in range(heads):
        prob = softmax(query[:, h * HEAD : (h + 1) * HEAD], keys, mask)
        attn[:, h * HEAD : (h + 1) * HEAD] = nn(prob.astype(BF16), values).astype(BF16)
    for k in reversed(range(count)):
        last[k].wait()
        outs[k][...] = nn(attn[...], wo[k]).astype(BF16)


def recompute_kernel(count, heads, *refs):
    xs, refs = refs[:count], refs[count:]
    gains, refs = refs[:count], refs[count:]
    wq_hbm, wkv_hbm, refs = *refs[:2], refs[2:]
    query_out, keyval_out, prob_out, inv_out, refs = *refs[:4], refs[4:]
    normed, wq, wkv, sems = refs
    col = lax.axis_index("tensor")
    first = load_rows(col, count, wq_hbm, wq, sems.at[0])
    first += load_rows(col, count, wkv_hbm, wkv, sems.at[1])
    inv = normalize(xs, gains, normed)
    inv_out[...] = jnp.broadcast_to(inv, inv_out.shape)
    for copy in first:
        copy.wait()
    keyval = nn(normed[...], wkv[...]).astype(BF16)
    query = nn(normed[...], wq[...]).astype(BF16)
    query_out[...] = query
    keyval_out[...] = keyval
    mask = causal_mask(query.shape[0])
    for h in range(heads):
        prob_out[h] = softmax(query[:, h * HEAD : (h + 1) * HEAD], keyval[:, :HEAD], mask)


def backward_kernel(count, heads, *refs):
    gs, refs = refs[:count], refs[count:]
    xs, refs = refs[:count], refs[count:]
    gains, refs = refs[:count], refs[count:]
    query, keyval, prob, wq_hbm, wkv_hbm, wo_hbm, refs = *refs[:6], refs[6:]
    outs, refs = refs[:count], refs[count:]
    total_out, refs = refs[0], refs[1:]
    wq, wkv, wo, d_query, sems = refs
    width = xs[0].shape[1]
    col = lax.axis_index("tensor")
    first = load_columns(col, count, wo_hbm, wo, sems.at[2])
    last = load_rows(col, count, wq_hbm, wq, sems.at[0])
    last += load_rows(col, count, wkv_hbm, wkv, sems.at[1])
    d_attn = None
    for k in range(count):
        first[k].wait()
        part = nt(gs[k][...], wo[k])
        d_attn = part if d_attn is None else d_attn + part
    d_attn = d_attn.astype(BF16)
    keys, values = keyval[:, :HEAD], keyval[:, HEAD:]
    d_key = d_value = None
    for h in range(heads):
        span = slice(h * HEAD, (h + 1) * HEAD)
        p = prob[h]
        d_head = d_attn[:, span]
        d_prob = nt(d_head, values)
        d_score = p * (d_prob - jnp.sum(p * d_prob, axis=-1, keepdims=True)) * SCALE
        d_score = d_score.astype(BF16)
        d_query[:, span] = nn(d_score, keys).astype(BF16)
        dk = tn(d_score, query[:, span])
        dv = tn(p.astype(BF16), d_head)
        d_key = dk if d_key is None else d_key + dk
        d_value = dv if d_value is None else d_value + dv
    d_pairs = jnp.concatenate([d_key.astype(BF16), d_value.astype(BF16)], axis=1)
    for copy in last:
        copy.wait()
    total = None
    for k in reversed(range(count)):
        rows = slice(k * width, (k + 1) * width)
        term = (nt(d_query[...], wq[rows, :]) + nt(d_pairs, wkv[rows, :])).astype(BF16)
        outs[k][...] = term
        scaled = term.astype(F32) * gains[k][...].astype(F32)
        part = jnp.sum(scaled * xs[k][...].astype(F32), axis=-1, keepdims=True)
        total = part if total is None else total + part
    total_out[...] = jnp.broadcast_to(total, total_out.shape)


def call(kernel, count, heads, ins, n_vmem, out_shape, scratch, flops, moved):
    return pl.pallas_call(
        functools.partial(kernel, count, heads),
        out_shape=out_shape,
        in_specs=[vmem_spec()] * n_vmem + [any_spec()] * (len(ins) - n_vmem),
        out_specs=[vmem_spec()] * len(out_shape),
        scratch_shapes=scratch,
        compiler_params=pltpu.CompilerParams(vmem_limit_bytes=48 * 2**20),
        cost_estimate=pl.CostEstimate(flops=flops, bytes_accessed=moved, transcendentals=0),
    )(*ins)


def local(
    embedded, outbox, loss_grad, grad_outbox, stash_held, norm_gain, w_query, w_keyval, w_out
):
    sections = lax.axis_size("section")
    count = lax.axis_size("tensor")
    position = lax.axis_index("section")
    held, grads_held, stash_held = outbox[0], grad_outbox[0], stash_held[0]
    seq, width = held.shape
    model = width * count
    wq, wkv, wo = w_query[0], w_keyval[0], w_out[0]
    qcols, kvcols = wq.shape[1], wkv.shape[1]
    heads = qcols // HEAD
    shape = jax.ShapeDtypeStruct

    block = sections // 4
    high = sections - block
    crossing = [s for s in range(sections - 1) if (s + 1) % block == 0]
    inside = [s for s in range(sections - 1) if (s + 1) % block]

    def send(value, pairs):
        return lax.ppermute(value, "section", pairs)

    arrived_inside = send(held, [(s, s + 1) for s in inside])
    arrived_crossing = send(held, [(s, s + 1) for s in crossing])
    fetched = send(stash_held, [(s, sections - 1 - s) for s in range(sections)])
    coming = send(grads_held, [(s + 1, s) for s in range(sections - 1)])
    evicted = send(held, [(s, sections - 2 - s) for s in range(high)])
    relayed = send(arrived_inside, [(s, sections - 1 - s) for s in range(high + 1, sections)])

    gains = gathered(norm_gain, "tensor")

    arrived = jnp.where(position % block == 0, arrived_crossing, arrived_inside)
    x_shard = jnp.where(position == 0, embedded, arrived)
    xs = gathered(x_shard, "tensor")
    weights = [
        pltpu.VMEM((model, qcols), BF16),
        pltpu.VMEM((model, kvcols), BF16),
    ]
    wo_buf = pltpu.VMEM((count, qcols, width), BF16)
    sems = pltpu.SemaphoreType.DMA((3, count))
    normed = pltpu.VMEM((seq, model), BF16)
    shares = [shape((seq, width), BF16)] * count
    proj = 2 * seq * model * (qcols + kvcols)
    out_flops = 2 * seq * model * qcols
    moved = 2 * model * (2 * qcols + kvcols)
    parts = call(
        forward_kernel, count, heads,
        [*xs, *gains, wq, wkv, wo], 2 * count, shares,
        [normed, *weights, wo_buf, pltpu.VMEM((seq, qcols), BF16), sems],
        proj + out_flops, moved,
    )
    mixed = reduced(parts, "tensor")
    section_out = (x_shard.astype(F32) + mixed).astype(BF16)

    bs = gathered(fetched, "tensor")
    query, keyval, prob, inv = call(
        recompute_kernel, count, heads,
        [*bs, *gains, wq, wkv], 2 * count,
        [
            shape((seq, qcols), BF16),
            shape((seq, kvcols), BF16),
            shape((heads, seq, seq), F32),
            shape((seq, HEAD), F32),
        ],
        [normed, *weights, sems],
        proj, moved,
    )
    g_shard = jnp.where(position == sections - 1, loss_grad, coming)
    gs = gathered(g_shard, "tensor")
    *terms, total = call(
        backward_kernel, count, heads,
        [*gs, *bs, *gains, query, keyval, prob, wq, wkv, wo], 3 * count + 3,
        [*shares, shape((seq, HEAD), F32)],
        [*weights, wo_buf, pltpu.VMEM((seq, qcols), BF16), sems],
        proj + out_flops, moved,
    )
    place, last, _ = lax.optimization_barrier((position, embedded, total))
    evicted = jnp.where(
        place < block - 1, relayed, jnp.where(place < sections - 1, evicted, last)
    )
    d_normed = reduced(terms, "tensor")
    total = sum(gathered(total, "tensor"))[:, :1]
    inv = inv[:, :1]
    scaled = d_normed * norm_gain.astype(F32)
    result = (
        g_shard.astype(F32) + inv * scaled - fetched.astype(F32) * inv**3 * (total / model)
    )
    return section_out[None], evicted[None], result.astype(BF16)[None]


def solution(mesh):
    return jax.shard_map(
        local,
        mesh=mesh,
        in_specs=(
            P(None, "tensor"),
            P("section", None, "tensor"),
            P(None, "tensor"),
            P("section", None, "tensor"),
            P("section", None, "tensor"),
            P("section", "tensor"),
            P("section", None, "tensor"),
            P("section", None, "tensor"),
            P("section", "tensor", None),
        ),
        out_specs=(
            P("section", None, "tensor"),
            P("section", None, "tensor"),
            P("section", None, "tensor"),
        ),
        check_vma=False,
    )
```

profile of v0, /device:TPU:17, one launch (start us, length us, event | category | flops | bytes accessed | tf_op | source)
XLA Modules:
  0.0 136.7 jit_solution(8837781507002674403)
XLA Ops:
  0.6 4.1 %collective-permute-start.1 = (bf16[256,2048]{1,0:T(8,128)(2,1)}, bf16[256,2048]{1,0:T(8,128)(2,1)}, u32[]{:S(2)}, u32[]{:S(2)}) collective-permute-start(bf16[256,2048]{1,0:T(8,128)(2,1)} %bitcast), channel_id=1, source_target_pairs={{0,2},{2,4},{4,6},{8,10},{10,12},{12,14},{16,18},{18,20},{20,22},{... | collective-permute-start | bytes 3145736 | tf_op jit(solution)/shard_map/ppermute | solution.py:241
  4.7 1.3 collective-permute-start
  6.0 4.0 %collective-permute-start.7 = (bf16[256,2048]{1,0:T(8,128)(2,1)}, bf16[256,2048]{1,0:T(8,128)(2,1)S(1)}, u32[]{:S(2)}, u32[]{:S(2)}) collective-permute-start(bf16[256,2048]{1,0:T(8,128)(2,1)} %bitcast.22), channel_id=1, source_target_pairs={{0,30},{2,28},{4,26},{6,24},{8,22},{10,20},{12,18},{14,16},{16,14}... | collective-permute-start | bytes 3145736 | tf_op jit(solution)/shard_map/ppermute | solution.py:241
  10.0 1.9 %collective-permute-start.5 = (bf16[256,2048]{1,0:T(8,128)(2,1)}, bf16[256,2048]{1,0:T(8,128)(2,1)}, u32[]{:S(2)}, u32[]{:S(2)}) collective-permute-start(bf16[256,2048]{1,0:T(8,128)(2,1)} %bitcast.23), channel_id=1, source_target_pairs={{2,0},{4,2},{6,4},{8,6},{10,8},{12,10},{14,12},{16,14},{18,16},{20... | collective-permute-start | bytes 3145736 | tf_op jit(solution)/shard_map/ppermute | solution.py:241
  12.0 14.0 %collective-permute-done.1 = bf16[256,2048]{1,0:T(8,128)(2,1)} collective-permute-done((bf16[256,2048]{1,0:T(8,128)(2,1)}, bf16[256,2048]{1,0:T(8,128)(2,1)}, u32[]{:S(2)}, u32[]{:S(2)}) %collective-permute-start.1) | collective-permute-done | bytes 1048608 | tf_op jit(solution)/shard_map/ppermute | solution.py:241
  26.0 6.4 %collective-permute-done = bf16[256,2048]{1,0:T(8,128)(2,1)S(1)} collective-permute-done((bf16[256,2048]{1,0:T(8,128)(2,1)}, bf16[256,2048]{1,0:T(8,128)(2,1)S(1)}, u32[]{:S(2)}, u32[]{:S(2)}) %collective-permute-start) | collective-permute-done | bytes 1048608 | tf_op jit(solution)/shard_map/ppermute | solution.py:241
  32.6 25.8 %collective-permute-start.2 = (bf16[256,2048]{1,0:T(8,128)(2,1)S(1)}, bf16[256,2048]{1,0:T(8,128)(2,1)S(1)}, u32[]{:S(2)}, u32[]{:S(2)}) collective-permute-start(bf16[256,2048]{1,0:T(8,128)(2,1)S(1)} %select_select_fusion.refs_0_), channel_id=1, source_target_pairs={{0,1},{1,0},{2,3},{3,2},{4,5},{5,4},{6,7},{7,6},{8,9},{9,8},{10,11... | collective-permute-start | bytes 3145736 | tf_op jit(solution)/shard_map/ppermute | solution.py:20
  58.4 19.0 %collective-permute-done.7.refs_0_.refs_2_ = bf16[256,2048]{1,0:T(8,128)(2,1)S(1)} collective-permute-done((bf16[256,2048]{1,0:T(8,128)(2,1)}, bf16[256,2048]{1,0:T(8,128)(2,1)S(1)}, u32[]{:S(2)}, u32[]{:S(2)}) %collective-permute-start.7) | collective-permute-done | bytes 1048608 | tf_op jit(solution)/shard_map/ppermute | solution.py:241
  77.4 1.8 %collective-permute-start.8 = (bf16[256,2048]{1,0:T(8,128)(2,1)S(1)}, bf16[256,2048]{1,0:T(8,128)(2,1)S(1)}, u32[]{:S(2)}, u32[]{:S(2)}) collective-permute-start(bf16[256,2048]{1,0:T(8,128)(2,1)S(1)} %collective-permute-done.7.refs_0_.refs_2_), channel_id=1, source_target_pairs={{0,1},{1,0},{2,3},{3,2},{4,5},{5,4},{6,7},{7,6},{8,9},{9,8},{10,11... | collective-permute-start | bytes 3145736 | tf_op jit(solution)/shard_map/ppermute | solution.py:20
  79.2 1.4 broadcast_select_fusion.refs_0_
  80.7 0.5 collective-permute-start.3
  81.1 1.9 %collective-permute-start.10 = (bf16[256,2048]{1,0:T(8,128)(2,1)}, bf16[256,2048]{1,0:T(8,128)(2,1)}, u32[]{:S(2)}, u32[]{:S(2)}) collective-permute-start(bf16[256,2048]{1,0:T(8,128)(2,1)} %bitcast), channel_id=1, source_target_pairs={{0,28},{2,26},{4,24},{6,22},{8,20},{10,18},{12,16},{14,14},{16,12}... | collective-permute-start | bytes 3145736 | tf_op jit(solution)/shard_map/ppermute | solution.py:241
  83.3 1.6 %collective-permute-start.9 = (bf16[256,2048]{1,0:T(8,128)(2,1)}, bf16[256,2048]{1,0:T(8,128)(2,1)}, u32[]{:S(2)}, u32[]{:S(2)}) collective-permute-start(bf16[256,2048]{1,0:T(8,128)(2,1)} %collective-permute-done.1), channel_id=1, source_target_pairs={{26,4},{28,2},{30,0},{27,5},{29,3},{31,1}} | collective-permute-start | bytes 3145736 | tf_op jit(solution)/shard_map/ppermute | solution.py:241
  85.0 9.4 %shard_map.112 = (bf16[256,2048]{1,0:T(8,128)(2,1)S(1)}, bf16[256,2048]{1,0:T(8,128)(2,1)}) custom-call(bf16[256,2048]{1,0:T(8,128)(2,1)S(1)} %select_select_fusion.refs_0_, bf16[256,2048]{1,0:T(8,128)(2,1)S(1)} %collective-permute-done.2.refs_1_, bf16[1,2048]{1,0:T(2,128)(2,1)S(1)} %copy-done.7, bf16[1,2048]{1,0:T(2,128)(2,1)S(1)} %collective-permute-done.3.refs_3_.refs_5_, ...), custom_call_target="tpu_custom_call" | custom-call | flops 2684354560 | bytes 10485760 | tf_op jit(solution)/shard_map/pallas_call | solution.py:210
  94.6 5.1 %shard_map.113 = (bf16[256,512]{1,0:T(8,128)(2,1)S(1)}, bf16[256,256]{1,0:T(8,128)(2,1)S(1)}, f32[4,256,256]{2,1,0:T(8,128)S(1)}, f32[256,128]{1,0:T(8,128)S(1)}) custom-call(bf16[256,2048]{1,0:T(8,128)(2,1)S(1)} %collective-permute-done.7.refs_0_.refs_2_, bf16[256,2048]{1,0:T(8,128)(2,1)S(1)} %collective-permute-done.8.refs_1_.refs_3_, ...), custom_call_target="tpu_custom_call" | custom-call | flops 1610612736 | bytes 10485760 | tf_op jit(solution)/shard_map/pallas_call | solution.py:210
  99.8 1.0 copy-done.2
  100.8 8.5 %shard_map.114 = (bf16[256,2048]{1,0:T(8,128)(2,1)S(1)}, bf16[256,2048]{1,0:T(8,128)(2,1)S(1)}, f32[256,128]{1,0:T(8,128)S(1)}) custom-call(bf16[256,2048]{1,0:T(8,128)(2,1)S(1)} %broadcast_select_fusion.refs_0_, bf16[256,2048]{1,0:T(8,128)(2,1)S(1)} %collective-permute-done.6.refs_1_, bf16[256,2048]{1,0:T(8,128)(2,1)S(1)} %collective-permute-done.7.refs_0_.refs_2_, ...), custom_call_target="tpu_custom_call" | custom-call | flops 2684354560 | bytes 10485760 | tf_op jit(solution)/shard_map/pallas_call | solution.py:210
  109.3 1.0 copy-done.5
  110.2 1.0 copy-done.8
  111.5 0.3 collective-permute-start.11
  111.8 17.6 %collective-permute-done.10 = bf16[256,2048]{1,0:T(8,128)(2,1)} collective-permute-done((bf16[256,2048]{1,0:T(8,128)(2,1)}, bf16[256,2048]{1,0:T(8,128)(2,1)}, u32[]{:S(2)}, u32[]{:S(2)}) %collective-permute-start.10) | collective-permute-done | bytes 1048608 | tf_op jit(solution)/shard_map/ppermute | solution.py:241
  129.4 2.3 %select_bitcast_fusion = bf16[1,256,2048]{2,1,0:T(8,128)(2,1)} fusion(bf16[256,2048]{1,0:T(8,128)(2,1)} %collective-permute-done.9, bf16[256,2048]{1,0:T(8,128)(2,1)} %collective-permute-done.10, bf16[256,2048]{1,0:T(8,128)(2,1)} %param.9, pred[]{:T(512)S(6)} %lt.14, pred[]{:T(512)S(6)} %lt.13), kind=kLoop, calls=%fused_computation.4 | loop fusion | flops 1048576 | bytes 4194306 | tf_op jit(solution)/shard_map/broadcast_in_dim | solution.py:308
  132.0 2.8 %fusion = bf16[1,256,2048]{2,1,0:T(8,128)(2,1)} fusion(bf16[256,2048]{1,0:T(8,128)(2,1)} %collective-permute-done.4, bf16[256,2048]{1,0:T(8,128)(2,1)S(1)} %copy-done.4, bf16[256,2048]{1,0:T(8,128)(2,1)S(1)} %select_select_fusion.refs_0_), kind=kLoop, calls=%fused_computation.2 | loop fusion | flops 3145728 | bytes 4194304 | tf_op jit(solution)/shard_map/broadcast_in_dim | solution.py:308
  134.9 1.9 %fusion.1 = bf16[1,256,2048]{2,1,0:T(8,128)(2,1)} fusion(bf16[256,2048]{1,0:T(8,128)(2,1)S(1)} %collective-permute-done.7.refs_0_.refs_2_, bf16[256,2048]{1,0:T(8,128)(2,1)S(1)} %collective-permute-done.11, bf16[256,2048]{1,0:T(8,128)(2,1)S(1)} %copy-done.6, bf16[256,2048]{1,0:T(8,128)(2,1)S(1)} %broadcast_select_fusion.refs_0_, f32[256]{0:T(256)S(1)} %fusion.4, ...), kind=kLoop, calls=%fused_computation.3 | loop fusion | flops 6291456 | bytes 5254144 | tf_op jit(solution)/shard_map/broadcast_in_dim | solution.py:308
  (33 shorter events, 1.2 us)
Async XLA Ops:
  0.6 25.4 %collective-permute-start.1 = (bf16[256,2048]{1,0:T(8,128)(2,1)}, bf16[256,2048]{1,0:T(8,128)(2,1)}, u32[]{:S(2)}, u32[]{:S(2)}) collective-permute-start(bf16[256,2048]{1,0:T(8,128)(2,1)} %bitcast), channel_id=1, source_target_pairs={{0,2},{2,4},{4,6},{8,10},{10,12},{12,14},{16,18},{18,20},{20,22},{... | collective-permute-start | bytes 3145736 | tf_op jit(solution)/shard_map/ppermute | solution.py:241
  4.7 27.7 %collective-permute-start = (bf16[256,2048]{1,0:T(8,128)(2,1)}, bf16[256,2048]{1,0:T(8,128)(2,1)S(1)}, u32[]{:S(2)}, u32[]{:S(2)}) collective-permute-start(bf16[256,2048]{1,0:T(8,128)(2,1)} %bitcast), channel_id=1, source_target_pairs={{6,8},{14,16},{22,24},{7,9},{15,17},{23,25}} | collective-permute-start | bytes 3145736 | tf_op jit(solution)/shard_map/ppermute | solution.py:241
  6.0 71.4 %collective-permute-start.7 = (bf16[256,2048]{1,0:T(8,128)(2,1)}, bf16[256,2048]{1,0:T(8,128)(2,1)S(1)}, u32[]{:S(2)}, u32[]{:S(2)}) collective-permute-start(bf16[256,2048]{1,0:T(8,128)(2,1)} %bitcast.22), channel_id=1, source_target_pairs={{0,30},{2,28},{4,26},{6,24},{8,22},{10,20},{12,18},{14,16},{16,14}... | collective-permute-start | bytes 3145736 | tf_op jit(solution)/shard_map/ppermute | solution.py:241
  10.0 69.2 %collective-permute-start.5 = (bf16[256,2048]{1,0:T(8,128)(2,1)}, bf16[256,2048]{1,0:T(8,128)(2,1)}, u32[]{:S(2)}, u32[]{:S(2)}) collective-permute-start(bf16[256,2048]{1,0:T(8,128)(2,1)} %bitcast.23), channel_id=1, source_target_pairs={{2,0},{4,2},{6,4},{8,6},{10,8},{12,10},{14,12},{16,14},{18,16},{20... | collective-permute-start | bytes 3145736 | tf_op jit(solution)/shard_map/ppermute | solution.py:241
  12.0 67.2 %copy-start.9 = (bf16[256,2048]{1,0:T(8,128)(2,1)S(1)}, bf16[256,2048]{1,0:T(8,128)(2,1)}, u32[]{:S(2)}) copy-start(bf16[256,2048]{1,0:T(8,128)(2,1)} %param.11) | copy-start | bytes 3145732
  32.6 48.1 %copy-start.7 = (bf16[1,2048]{1,0:T(2,128)(2,1)S(1)}, bf16[1,2048]{1,0:T(2,128)(2,1)}, u32[]{:S(2)}) copy-start(bf16[1,2048]{1,0:T(2,128)(2,1)} %refs_4_.1) | copy-start | bytes 12292
  32.6 52.3 %collective-permute-start.2 = (bf16[256,2048]{1,0:T(8,128)(2,1)S(1)}, bf16[256,2048]{1,0:T(8,128)(2,1)S(1)}, u32[]{:S(2)}, u32[]{:S(2)}) collective-permute-start(bf16[256,2048]{1,0:T(8,128)(2,1)S(1)} %select_select_fusion.refs_0_), channel_id=1, source_target_pairs={{0,1},{1,0},{2,3},{3,2},{4,5},{5,4},{6,7},{7,6},{8,9},{9,8},{10,11... | collective-permute-start | bytes 3145736 | tf_op jit(solution)/shard_map/ppermute | solution.py:20
  77.4 17.3 %collective-permute-start.8 = (bf16[256,2048]{1,0:T(8,128)(2,1)S(1)}, bf16[256,2048]{1,0:T(8,128)(2,1)S(1)}, u32[]{:S(2)}, u32[]{:S(2)}) collective-permute-start(bf16[256,2048]{1,0:T(8,128)(2,1)S(1)} %collective-permute-done.7.refs_0_.refs_2_), channel_id=1, source_target_pairs={{0,1},{1,0},{2,3},{3,2},{4,5},{5,4},{6,7},{7,6},{8,9},{9,8},{10,11... | collective-permute-start | bytes 3145736 | tf_op jit(solution)/shard_map/ppermute | solution.py:20
  80.6 20.2 %collective-permute-start.6 = (bf16[256,2048]{1,0:T(8,128)(2,1)S(1)}, bf16[256,2048]{1,0:T(8,128)(2,1)S(1)}, u32[]{:S(2)}, u32[]{:S(2)}) collective-permute-start(bf16[256,2048]{1,0:T(8,128)(2,1)S(1)} %broadcast_select_fusion.refs_0_), channel_id=1, source_target_pairs={{0,1},{1,0},{2,3},{3,2},{4,5},{5,4},{6,7},{7,6},{8,9},{9,8},{10,11... | collective-permute-start | bytes 3145736 | tf_op jit(solution)/shard_map/ppermute | solution.py:20
  80.7 2.6 %collective-permute-start.3 = (bf16[1,2048]{1,0:T(2,128)(2,1)S(1)}, bf16[1,2048]{1,0:T(2,128)(2,1)S(1)}, u32[]{:S(2)}, u32[]{:S(2)}) collective-permute-start(bf16[1,2048]{1,0:T(2,128)(2,1)S(1)} %copy-done.7), channel_id=1, source_target_pairs={{0,1},{1,0},{2,3},{3,2},{4,5},{5,4},{6,7},{7,6},{8,9},{9,8},{10,11... | collective-permute-start | bytes 12296 | tf_op jit(solution)/shard_map/ppermute | solution.py:20
  81.1 48.3 %collective-permute-start.10 = (bf16[256,2048]{1,0:T(8,128)(2,1)}, bf16[256,2048]{1,0:T(8,128)(2,1)}, u32[]{:S(2)}, u32[]{:S(2)}) collective-permute-start(bf16[256,2048]{1,0:T(8,128)(2,1)} %bitcast), channel_id=1, source_target_pairs={{0,28},{2,26},{4,24},{6,22},{8,20},{10,18},{12,16},{14,14},{16,12}... | collective-permute-start | bytes 3145736 | tf_op jit(solution)/shard_map/ppermute | solution.py:241
  83.3 46.1 %collective-permute-start.9 = (bf16[256,2048]{1,0:T(8,128)(2,1)}, bf16[256,2048]{1,0:T(8,128)(2,1)}, u32[]{:S(2)}, u32[]{:S(2)}) collective-permute-start(bf16[256,2048]{1,0:T(8,128)(2,1)} %collective-permute-done.1), channel_id=1, source_target_pairs={{26,4},{28,2},{30,0},{27,5},{29,3},{31,1}} | collective-permute-start | bytes 3145736 | tf_op jit(solution)/shard_map/ppermute | solution.py:241
  85.0 9.7 %copy-start = (bf16[1,4096,256]{2,1,0:T(8,128)(2,1)S(1)}, bf16[1,4096,256]{2,1,0:T(8,128)(2,1)}, u32[]{:S(2)}) copy-start(bf16[1,4096,256]{2,1,0:T(8,128)(2,1)} %param.16) | copy-start | bytes 6291460
  94.4 5.3 %copy-start.3 = (bf16[256,2048]{1,0:T(8,128)(2,1)}, bf16[256,2048]{1,0:T(8,128)(2,1)S(1)}, u32[]{:S(2)}) copy-start(bf16[256,2048]{1,0:T(8,128)(2,1)S(1)} %get-tuple-element.14) | copy-start | bytes 3145732
  94.4 37.6 %collective-permute-start.4 = (bf16[256,2048]{1,0:T(8,128)(2,1)}, bf16[256,2048]{1,0:T(8,128)(2,1)}, u32[]{:S(2)}, u32[]{:S(2)}) collective-permute-start(bf16[256,2048]{1,0:T(8,128)(2,1)} %get-tuple-element.15), channel_id=1, source_target_pairs={{0,1},{1,0},{2,3},{3,2},{4,5},{5,4},{6,7},{7,6},{8,9},{9,8},{10,11... | collective-permute-start | bytes 3145736 | tf_op jit(solution)/shard_map/ppermute | solution.py:20
  94.6 5.1 %copy-start.1 = (bf16[256,2048]{1,0:T(8,128)(2,1)}, bf16[256,2048]{1,0:T(8,128)(2,1)S(1)}, u32[]{:S(2)}) copy-start(bf16[256,2048]{1,0:T(8,128)(2,1)S(1)} %collective-permute-done.8.refs_1_.refs_3_) | copy-start | bytes 3145732
  99.8 1.0 copy-start.2
  109.3 1.0 copy-start.5
  110.2 1.0 copy-start.8
  111.3 20.6 %collective-permute-start.12 = (f32[256,128]{1,0:T(8,128)S(1)}, f32[256,128]{1,0:T(8,128)S(1)}, u32[]{:S(2)}, u32[]{:S(2)}) collective-permute-start(f32[256,128]{1,0:T(8,128)S(1)} %get-tuple-element.19), channel_id=1, source_target_pairs={{0,1},{1,0},{2,3},{3,2},{4,5},{5,4},{6,7},{7,6},{8,9},{9,8},{10,11... | collective-permute-start | bytes 393224 | tf_op jit(solution)/shard_map/ppermute | solution.py:20
  111.5 20.6 %copy-start.4 = (bf16[256,2048]{1,0:T(8,128)(2,1)S(1)}, bf16[256,2048]{1,0:T(8,128)(2,1)}, u32[]{:S(2)}) copy-start(bf16[256,2048]{1,0:T(8,128)(2,1)} %copy-done.3) | copy-start | bytes 3145732
  111.5 23.4 %collective-permute-start.11 = (bf16[256,2048]{1,0:T(8,128)(2,1)}, bf16[256,2048]{1,0:T(8,128)(2,1)S(1)}, u32[]{:S(2)}, u32[]{:S(2)}) collective-permute-start(bf16[256,2048]{1,0:T(8,128)(2,1)} %copy-done.8), channel_id=1, source_target_pairs={{0,1},{1,0},{2,3},{3,2},{4,5},{5,4},{6,7},{7,6},{8,9},{9,8},{10,11... | collective-permute-start | bytes 3145736 | tf_op jit(solution)/shard_map/ppermute | solution.py:20
  132.0 2.8 %copy-start.6 = (bf16[256,2048]{1,0:T(8,128)(2,1)S(1)}, bf16[256,2048]{1,0:T(8,128)(2,1)}, u32[]{:S(2)}) copy-start(bf16[256,2048]{1,0:T(8,128)(2,1)} %copy-done.5) | copy-start | bytes 3145732
where the time goes:
time: 138 us; the launch traced here: 137 us
  waiting for transfers between devices  57.4 us (42%)
  starting transfers between devices  43.7 us (32%)
  Pallas kernels  23 us (17%)
  other arithmetic  8.79 us (6%)
  local copies, waits for them, and re-layouts  2.98 us (2%)
    ppermute x6, waiting for transfers between devices, send(): return lax.ppermute(value, 'section', pairs)  57.1 us
    ppermute x7, starting transfers between devices, rotate(): lax.ppermute(value, axis, [(i, (i - k) % count) for i in range(count)])  28.9 us
    pallas_call x3, Pallas kernels, call(): pl.pallas_call(functools.partial(kernel, count, heads), out_shape=out_sha...  23 us
    ppermute x6, starting transfers between devices, send(): return lax.ppermute(value, 'section', pairs)  14.9 us
    broadcast_in_dim x3, other arithmetic, local(): return (section_out[None], evicted[None], result.astype(BF16)[None])  7 us
    unnamed x20, local copies, waits for them, and re-layouts  2.98 us
  transfers between devices with their start and end apart: 13, of which 5 were waited for; matrix products, arithmetic and copies ran while one was open for 5% of the time, Pallas kernels for 17%

commit v1 on v0

v1 whole, which is shorter than its diff:
```python
import functools

import jax
import jax.numpy as jnp
from jax import lax
from jax.experimental import pallas as pl
from jax.experimental.pallas import tpu as pltpu
from jax.sharding import PartitionSpec as P


HEAD = 128
EPS = 1e-05
SCALE = HEAD ** (-0.5)
F32 = jnp.float32
BF16 = jnp.bfloat16

LIMIT = 14 * 2**20


def rotate(value, axis, k):
    count = lax.axis_size(axis)
    return lax.ppermute(value, axis, [(i, (i - k) % count) for i in range(count)])


def gathered(value, axis):
    return [value] + [rotate(value, axis, k) for k in range(1, lax.axis_size(axis))]


def reduced(parts, axis):
    total = parts[0].astype(F32)
    for k in range(1, len(parts)):
        total = total + rotate(parts[k], axis, -k).astype(F32)
    return total


def nt(a, b):
    return lax.dot_general(a, b, (((1,), (1,)), ((), ())), preferred_element_type=F32)


def tn(a, b):
    return lax.dot_general(a, b, (((0,), (0,)), ((), ())), preferred_element_type=F32)


def nn(a, b):
    return jnp.dot(a, b, preferred_element_type=F32)


def vmem_spec():
    return pl.BlockSpec(memory_space=pltpu.VMEM)


def rows_of(ref, col, k, count):
    width = ref.shape[0] // count
    return ref[pl.ds(pl.multiple_of(lax.rem(col + k, count) * width, width), width), :]


def columns_of(ref, col, k, count):
    width = ref.shape[1] // count
    return ref[:, pl.ds(pl.multiple_of(lax.rem(col + k, count) * width, width), width)]


def project(normed, weights, col, count):
    width = weights.shape[0] // count
    total = None
    for k in range(count):
        part = nn(normed[:, k * width : (k + 1) * width], rows_of(weights, col, k, count))
        total = part if total is None else total + part
    return total.astype(BF16)


def normalize(xs, gains, normed):
    width = xs[0].shape[1]
    total = None
    for x in xs:
        xf = x[...].astype(F32)
        part = jnp.sum(xf * xf, axis=-1, keepdims=True)
        total = part if total is None else total + part
    inv = lax.rsqrt(total / (width * len(xs)) + EPS)
    for k, x in enumerate(xs):
        xf = x[...].astype(F32)
        normed[:, k * width : (k + 1) * width] = (xf * inv * gains[k][...].astype(F32)).astype(BF16)
    return inv


def causal_mask(seq):
    rows = lax.broadcasted_iota(jnp.int32, (seq, seq), 0)
    cols = lax.broadcasted_iota(jnp.int32, (seq, seq), 1)
    return rows >= cols


def softmax(query, keys, mask):
    scores = jnp.where(mask, nt(query, keys) * SCALE, -1e30)
    top = jnp.max(scores, axis=-1, keepdims=True)
    weights = jnp.exp(scores - top)
    return weights / jnp.sum(weights, axis=-1, keepdims=True)


def forward_kernel(count, heads, *refs):
    xs, refs = refs[:count], refs[count:]
    gains, refs = refs[:count], refs[count:]
    wq, wkv, wo, refs = *refs[:3], refs[3:]
    outs, (normed, attn) = refs[:count], refs[count:]
    col = lax.axis_index("tensor")
    normalize(xs, gains, normed)
    keyval = project(normed, wkv, col, count)
    query = project(normed, wq, col, count)
    keys, values = keyval[:, :HEAD], keyval[:, HEAD:]
    mask = causal_mask(query.shape[0])
    for h in range(heads):
        prob = softmax(query[:, h * HEAD : (h + 1) * HEAD], keys, mask)
        attn[:, h * HEAD : (h + 1) * HEAD] = nn(prob.astype(BF16), values).astype(BF16)
    for k in reversed(range(count)):
        outs[k][...] = nn(attn[...], columns_of(wo, col, k, count)).astype(BF16)


def recompute_kernel(count, heads, *refs):
    xs, refs = refs[:count], refs[count:]
    gains, refs = refs[:count], refs[count:]
    wq, wkv, query_out, keyval_out, prob_out, inv_out, normed = refs
    col = lax.axis_index("tensor")
    inv = normalize(xs, gains, normed)
    inv_out[...] = jnp.broadcast_to(inv, inv_out.shape)
    keyval = project(normed, wkv, col, count)
    query = project(normed, wq, col, count)
    query_out[...] = query
    keyval_out[...] = keyval
    mask = causal_mask(query.shape[0])
    for h in range(heads):
        prob_out[h] = softmax(query[:, h * HEAD : (h + 1) * HEAD], keyval[:, :HEAD], mask)


def backward_kernel(count, heads, *refs):
    gs, refs = refs[:count], refs[count:]
    xs, refs = refs[:count], refs[count:]
    gains, refs = refs[:count], refs[count:]
    query, keyval, prob, wq, wkv, wo, refs = *refs[:6], refs[6:]
    outs, (total_out, d_query) = refs[:count], refs[count:]
    col = lax.axis_index("tensor")
    d_attn = None
    for k in range(count):
        part = nt(gs[k][...], columns_of(wo, col, k, count))
        d_attn = part if d_attn is None else d_attn + part
    d_attn = d_attn.astype(BF16)
    keys, values = keyval[:, :HEAD], keyval[:, HEAD:]
    d_key = d_value = None
    for h in range(heads):
        span = slice(h * HEAD, (h + 1) * HEAD)
        p = prob[h]
        d_head = d_attn[:, span]
        d_prob = nt(d_head, values)
        d_score = p * (d_prob - jnp.sum(p * d_prob, axis=-1, keepdims=True)) * SCALE
        d_score = d_score.astype(BF16)
        d_query[:, span] = nn(d_score, keys).astype(BF16)
        dk = tn(d_score, query[:, span])
        dv = tn(p.astype(BF16), d_head)
        d_key = dk if d_key is None else d_key + dk
        d_value = dv if d_value is None else d_value + dv
    d_pairs = jnp.concatenate([d_key.astype(BF16), d_value.astype(BF16)], axis=1)
    total = None
    for k in reversed(range(count)):
        term = nt(d_query[...], rows_of(wq, col, k, count))
        term = (term + nt(d_pairs, rows_of(wkv, col, k, count))).astype(BF16)
        outs[k][...] = term
        scaled = term.astype(F32) * gains[k][...].astype(F32)
        part = jnp.sum(scaled * xs[k][...].astype(F32), axis=-1, keepdims=True)
        total = part if total is None else total + part
    total_out[...] = jnp.broadcast_to(total, total_out.shape)


def call(kernel, count, heads, ins, out_shape, scratch, flops, moved):
    return pl.pallas_call(
        functools.partial(kernel, count, heads),
        out_shape=out_shape,
        in_specs=[vmem_spec()] * len(ins),
        out_specs=[vmem_spec()] * len(out_shape),
        scratch_shapes=scratch,
        compiler_params=pltpu.CompilerParams(vmem_limit_bytes=LIMIT),
        cost_estimate=pl.CostEstimate(flops=flops, bytes_accessed=moved, transcendentals=0),
    )(*ins)


def local(
    embedded, outbox, loss_grad, grad_outbox, stash_held, norm_gain, w_query, w_keyval, w_out
):
    sections = lax.axis_size("section")
    count = lax.axis_size("tensor")
    position = lax.axis_index("section")
    held, grads_held, stash_held = outbox[0], grad_outbox[0], stash_held[0]
    seq, width = held.shape
    model = width * count
    wq, wkv, wo = w_query[0], w_keyval[0], w_out[0]
    qcols, kvcols = wq.shape[1], wkv.shape[1]
    heads = qcols // HEAD
    shape = jax.ShapeDtypeStruct

    block = sections // 4
    high = sections - block
    near, far = range(block, high), [*range(block), *range(high, sections)]

    def send(value, pairs):
        return lax.ppermute(value, "section", pairs)

    fetched_near = send(stash_held, [(s, sections - 1 - s) for s in near])
    arrived = send(held, [(s, s + 1) for s in range(sections - 1)])
    coming = send(grads_held, [(s + 1, s) for s in range(sections - 1)])
    evicted_near = send(held, [(s, sections - 2 - s) for s in near])
    fetched_far = send(stash_held, [(s, sections - 1 - s) for s in far])
    evicted_far = send(held, [(s, sections - 2 - s) for s in range(block)])
    relayed = send(arrived, [(s, sections - 1 - s) for s in range(high + 1, sections)])
    fetched = jnp.where((position >= block) & (position < high), fetched_near, fetched_far)

    gains = gathered(norm_gain, "tensor")

    x_shard = jnp.where(position == 0, embedded, arrived)
    xs = gathered(x_shard, "tensor")
    normed = pltpu.VMEM((seq, model), BF16)
    shares = [shape((seq, width), BF16)] * count
    proj = 2 * seq * model * (qcols + kvcols)
    out_flops = 2 * seq * model * qcols
    moved = 2 * model * (2 * qcols + kvcols)
    parts = call(
        forward_kernel, count, heads,
        [*xs, *gains, wq, wkv, wo], shares,
        [normed, pltpu.VMEM((seq, qcols), BF16)],
        proj + out_flops, moved,
    )
    mixed = reduced(parts, "tensor")
    section_out = (x_shard.astype(F32) + mixed).astype(BF16)

    bs = gathered(fetched, "tensor")
    query, keyval, prob, inv = call(
        recompute_kernel, count, heads,
        [*bs, *gains, wq, wkv],
        [
            shape((seq, qcols), BF16),
            shape((seq, kvcols), BF16),
            shape((heads, seq, seq), F32),
            shape((seq, HEAD), F32),
        ],
        [normed],
        proj, moved,
    )
    g_shard = jnp.where(position == sections - 1, loss_grad, coming)
    gs = gathered(g_shard, "tensor")
    *terms, total = call(
        backward_kernel, count, heads,
        [*gs, *bs, *gains, query, keyval, prob, wq, wkv, wo],
        [*shares, shape((seq, HEAD), F32)],
        [pltpu.VMEM((seq, qcols), BF16)],
        proj + out_flops, moved,
    )
    place, last, _ = lax.optimization_barrier((position, embedded, total))
    evicted = jnp.where(
        place < block - 1,
        relayed,
        jnp.where(
            place < high - 1, evicted_near, jnp.where(place < sections - 1, evicted_far, last)
        ),
    )
    d_normed = reduced(terms, "tensor")
    total = sum(gathered(total, "tensor"))[:, :1]
    inv = inv[:, :1]
    scaled = d_normed * norm_gain.astype(F32)
    result = (
        g_shard.astype(F32) + inv * scaled - fetched.astype(F32) * inv**3 * (total / model)
    )
    return section_out[None], evicted[None], result.astype(BF16)[None]


def solution(mesh):
    return jax.shard_map(
        local,
        mesh=mesh,
        in_specs=(
            P(None, "tensor"),
            P("section", None, "tensor"),
            P(None, "tensor"),
            P("section", None, "tensor"),
            P("section", None, "tensor"),
            P("section", "tensor"),
            P("section", None, "tensor"),
            P("section", None, "tensor"),
            P("section", "tensor", None),
        ),
        out_specs=(
            P("section", None, "tensor"),
            P("section", None, "tensor"),
            P("section", None, "tensor"),
        ),
        check_vma=False,
    )
```

time: 138 us -> 138 us (level)
  the two profiles are of different devices: /device:TPU:17 before, /device:TPU:7 now
where the time goes in v1:
time: 138 us; the launch traced here: 137 us
  waiting for transfers between devices  62.1 us (45%)
  starting transfers between devices  45.3 us (33%)
  Pallas kernels  13.4 us (10%)
  other arithmetic  10.6 us (8%)
  local copies, waits for them, and re-layouts  5.18 us (4%)
    ppermute x7, waiting for transfers between devices, send(): return lax.ppermute(value, 'section', pairs)  61.1 us
    ppermute x7, starting transfers between devices, send(): return lax.ppermute(value, 'section', pairs)  39.5 us
    pallas_call x3, Pallas kernels, call(): pl.pallas_call(functools.partial(kernel, count, heads), out_shape=out_sha...  13.4 us
    broadcast_in_dim x3, other arithmetic, local(): return (section_out[None], evicted[None], result.astype(BF16)[None])  7.39 us
    ppermute x7, starting transfers between devices, rotate(): lax.ppermute(value, axis, [(i, (i - k) % count) for i in range(count)])  5.78 us
    unnamed x22, local copies, waits for them, and re-layouts  5.18 us
  transfers between devices with their start and end apart: 14, of which 4 were waited for; matrix products, arithmetic and copies ran while one was open for 6% of the time, Pallas kernels for 10%

profile of v1, /device:TPU:7, one launch (start us, length us, event | category | flops | bytes accessed | tf_op | source)
XLA Modules:
  0.0 137.4 jit_solution(14130949456340768238)
XLA Ops:
  0.6 3.1 %collective-permute-start = (bf16[256,2048]{1,0:T(8,128)(2,1)}, bf16[256,2048]{1,0:T(8,128)(2,1)S(1)}, u32[]{:S(2)}, u32[]{:S(2)}) collective-permute-start(bf16[256,2048]{1,0:T(8,128)(2,1)} %bitcast), channel_id=1, source_target_pairs={{0,2},{2,4},{4,6},{6,8},{8,10},{10,12},{12,14},{14,16},{16,18},{18... | collective-permute-start | bytes 3145736 | tf_op jit(solution)/shard_map/ppermute | solution.py:201
  4.5 5.1 %collective-permute-start.7 = (bf16[256,2048]{1,0:T(8,128)(2,1)}, bf16[256,2048]{1,0:T(8,128)(2,1)}, u32[]{:S(2)}, u32[]{:S(2)}) collective-permute-start(bf16[256,2048]{1,0:T(8,128)(2,1)} %bitcast.23), channel_id=1, source_target_pairs={{0,30},{2,28},{4,26},{6,24},{24,6},{26,4},{28,2},{30,0},{1,31},{3,... | collective-permute-start | bytes 3145736 | tf_op jit(solution)/shard_map/ppermute | solution.py:201
  9.6 3.1 %collective-permute-start.4 = (bf16[256,2048]{1,0:T(8,128)(2,1)}, bf16[256,2048]{1,0:T(8,128)(2,1)}, u32[]{:S(2)}, u32[]{:S(2)}) collective-permute-start(bf16[256,2048]{1,0:T(8,128)(2,1)} %bitcast.24), channel_id=1, source_target_pairs={{2,0},{4,2},{6,4},{8,6},{10,8},{12,10},{14,12},{16,14},{18,16},{20... | collective-permute-start | bytes 3145736 | tf_op jit(solution)/shard_map/ppermute | solution.py:201
  12.8 36.6 %collective-permute-done = bf16[256,2048]{1,0:T(8,128)(2,1)S(1)} collective-permute-done((bf16[256,2048]{1,0:T(8,128)(2,1)}, bf16[256,2048]{1,0:T(8,128)(2,1)S(1)}, u32[]{:S(2)}, u32[]{:S(2)}) %collective-permute-start) | collective-permute-done | bytes 1048608 | tf_op jit(solution)/shard_map/ppermute | solution.py:201
  49.5 2.6 %collective-permute-start.1 = (bf16[256,2048]{1,0:T(8,128)(2,1)S(1)}, bf16[256,2048]{1,0:T(8,128)(2,1)S(1)}, u32[]{:S(2)}, u32[]{:S(2)}) collective-permute-start(bf16[256,2048]{1,0:T(8,128)(2,1)S(1)} %broadcast_select_fusion.2.refs_0_), channel_id=1, source_target_pairs={{0,1},{1,0},{2,3},{3,2},{4,5},{5,4},{6,7},{7,6},{8,9},{9,8},{10,11... | collective-permute-start | bytes 3145736 | tf_op jit(solution)/shard_map/ppermute | solution.py:22
  52.1 1.5 %broadcast_select_fusion.refs_0_.refs_2_ = bf16[256,2048]{1,0:T(8,128)(2,1)S(1)} fusion(bf16[256,2048]{1,0:T(8,128)(2,1)S(1)} %collective-permute-done.6, bf16[256,2048]{1,0:T(8,128)(2,1)} %collective-permute-done.7, pred[]{:T(512)S(6)} %and.4), kind=kLoop, calls=%fused_computation.5 | loop fusion | flops 524288 | bytes 3145729 | tf_op jit(solution)/shard_map/jit(_where)/select_n | solution.py:210
  54.5 3.5 %collective-permute-done.4 = bf16[256,2048]{1,0:T(8,128)(2,1)} collective-permute-done((bf16[256,2048]{1,0:T(8,128)(2,1)}, bf16[256,2048]{1,0:T(8,128)(2,1)}, u32[]{:S(2)}, u32[]{:S(2)}) %collective-permute-start.4) | collective-permute-done | bytes 1048608 | tf_op jit(solution)/shard_map/ppermute | solution.py:201
  58.0 1.3 broadcast_select_fusion.1.refs_0_
  59.9 1.3 collective-permute-start.10
  61.2 0.9 collective-permute-done.2.refs_3_.refs_5_
  62.2 24.5 %collective-permute-start.11 = (bf16[256,2048]{1,0:T(8,128)(2,1)}, bf16[256,2048]{1,0:T(8,128)(2,1)}, u32[]{:S(2)}, u32[]{:S(2)}) collective-permute-start(bf16[256,2048]{1,0:T(8,128)(2,1)} %bitcast), channel_id=1, source_target_pairs={{0,28},{2,26},{4,24},{6,22},{1,29},{3,27},{5,25},{7,23}} | collective-permute-start | bytes 3145736 | tf_op jit(solution)/shard_map/ppermute | solution.py:201
  86.7 1.6 %collective-permute-start.9 = (bf16[256,2048]{1,0:T(8,128)(2,1)}, bf16[256,2048]{1,0:T(8,128)(2,1)}, u32[]{:S(2)}, u32[]{:S(2)}) collective-permute-start(bf16[256,2048]{1,0:T(8,128)(2,1)} %copy-done.10), channel_id=1, source_target_pairs={{26,4},{28,2},{30,0},{27,5},{29,3},{31,1}} | collective-permute-start | bytes 3145736 | tf_op jit(solution)/shard_map/ppermute | solution.py:201
  88.3 2.2 %copy-done.2 = bf16[1,512,4096]{2,1,0:T(8,128)(2,1)S(1)} copy-done((bf16[1,512,4096]{2,1,0:T(8,128)(2,1)S(1)}, bf16[1,512,4096]{2,1,0:T(8,128)(2,1)}, u32[]{:S(2)}) %copy-start.2) | copy-done | bytes 4194328
  90.5 5.8 %shard_map.112 = (bf16[256,2048]{1,0:T(8,128)(2,1)S(1)}, bf16[256,2048]{1,0:T(8,128)(2,1)}) custom-call(bf16[256,2048]{1,0:T(8,128)(2,1)S(1)} %broadcast_select_fusion.2.refs_0_, bf16[256,2048]{1,0:T(8,128)(2,1)S(1)} %collective-permute-done.1.refs_1_, bf16[1,2048]{1,0:T(2,128)(2,1)S(1)} %copy-done.7, ...), custom_call_target="tpu_custom_call" | custom-call | flops 2684354560 | bytes 10485760 | tf_op jit(solution)/shard_map/pallas_call | solution.py:171
  96.3 1.0 copy-done.3
  98.0 2.8 %shard_map.113 = (bf16[256,512]{1,0:T(8,128)(2,1)S(1)}, bf16[256,256]{1,0:T(8,128)(2,1)S(1)}, f32[4,256,256]{2,1,0:T(8,128)S(1)}, f32[256,128]{1,0:T(8,128)S(1)}) custom-call(bf16[256,2048]{1,0:T(8,128)(2,1)S(1)} %broadcast_select_fusion.refs_0_.refs_2_, bf16[256,2048]{1,0:T(8,128)(2,1)S(1)} %collective-permute-done.8.refs_1_.refs_3_, ...), custom_call_target="tpu_custom_call" | custom-call | flops 1610612736 | bytes 10485760 | tf_op jit(solution)/shard_map/pallas_call | solution.py:171
  100.8 4.7 %shard_map.114 = (bf16[256,2048]{1,0:T(8,128)(2,1)S(1)}, bf16[256,2048]{1,0:T(8,128)(2,1)S(1)}, f32[256,128]{1,0:T(8,128)S(1)}) custom-call(bf16[256,2048]{1,0:T(8,128)(2,1)S(1)} %broadcast_select_fusion.1.refs_0_, bf16[256,2048]{1,0:T(8,128)(2,1)S(1)} %collective-permute-done.5.refs_1_, bf16[256,2048]{1,0:T(8,128)(2,1)S(1)} %broadcast_select_fusion.refs_0_.refs_2_, ...), custom_call_target="tpu_custom_call" | custom-call | flops 2684354560 | bytes 10485760 | tf_op jit(solution)/shard_map/pallas_call | solution.py:171
  105.6 1.0 copy-done.5
  106.6 1.0 copy-done.8
  107.6 21.1 %collective-permute-done.10 = bf16[256,2048]{1,0:T(8,128)(2,1)} collective-permute-done((bf16[256,2048]{1,0:T(8,128)(2,1)}, bf16[256,2048]{1,0:T(8,128)(2,1)}, u32[]{:S(2)}, u32[]{:S(2)}) %collective-permute-start.10) | collective-permute-done | bytes 1048608 | tf_op jit(solution)/shard_map/ppermute | solution.py:201
  128.7 1.0 collective-permute-start.12
  129.7 2.7 %select_bitcast_fusion = bf16[1,256,2048]{2,1,0:T(8,128)(2,1)} fusion(bf16[256,2048]{1,0:T(8,128)(2,1)} %collective-permute-done.9, bf16[256,2048]{1,0:T(8,128)(2,1)} %collective-permute-done.10, bf16[256,2048]{1,0:T(8,128)(2,1)} %collective-permute-done.11, bf16[256,2048]{1,0:T(8,128)(2,1)} %param.9, pred[]{:T(512)S(6)} %lt.15, pred[]{:T(512)S(6)} %lt.14, ...), kind=kLoop, calls=%fused_computation.4 | loop fusion | flops 1572864 | bytes 5242883 | tf_op jit(solution)/shard_map/broadcast_in_dim | solution.py:267
  132.7 2.8 %fusion = bf16[1,256,2048]{2,1,0:T(8,128)(2,1)} fusion(bf16[256,2048]{1,0:T(8,128)(2,1)} %collective-permute-done.3, bf16[256,2048]{1,0:T(8,128)(2,1)S(1)} %copy-done.4, bf16[256,2048]{1,0:T(8,128)(2,1)S(1)} %broadcast_select_fusion.2.refs_0_), kind=kLoop, calls=%fused_computation.2 | loop fusion | flops 3145728 | bytes 4194304 | tf_op jit(solution)/shard_map/broadcast_in_dim | solution.py:267
  135.5 1.9 %fusion.1 = bf16[1,256,2048]{2,1,0:T(8,128)(2,1)} fusion(bf16[256,2048]{1,0:T(8,128)(2,1)S(1)} %broadcast_select_fusion.refs_0_.refs_2_, bf16[256,2048]{1,0:T(8,128)(2,1)S(1)} %collective-permute-done.12, bf16[256,2048]{1,0:T(8,128)(2,1)S(1)} %copy-done.6, bf16[256,2048]{1,0:T(8,128)(2,1)S(1)} %broadcast_select_fusion.1.refs_0_, f32[256]{0:T(256)S(1)} %fusion.4, ...), kind=kLoop, calls=%fused_computation.3 | loop fusion | flops 6291456 | bytes 5254144 | tf_op jit(solution)/shard_map/broadcast_in_dim | solution.py:267
  (38 shorter events, 3.3 us)
Async XLA Ops:
  0.6 48.7 %collective-permute-start = (bf16[256,2048]{1,0:T(8,128)(2,1)}, bf16[256,2048]{1,0:T(8,128)(2,1)S(1)}, u32[]{:S(2)}, u32[]{:S(2)}) collective-permute-start(bf16[256,2048]{1,0:T(8,128)(2,1)} %bitcast), channel_id=1, source_target_pairs={{0,2},{2,4},{4,6},{6,8},{8,10},{10,12},{12,14},{14,16},{16,18},{18... | collective-permute-start | bytes 3145736 | tf_op jit(solution)/shard_map/ppermute | solution.py:201
  3.8 48.3 %collective-permute-start.6 = (bf16[256,2048]{1,0:T(8,128)(2,1)}, bf16[256,2048]{1,0:T(8,128)(2,1)S(1)}, u32[]{:S(2)}, u32[]{:S(2)}) collective-permute-start(bf16[256,2048]{1,0:T(8,128)(2,1)} %bitcast.22), channel_id=1, source_target_pairs={{8,22},{10,20},{12,18},{14,16},{16,14},{18,12},{20,10},{22,8},{9,2... | collective-permute-start | bytes 3145736 | tf_op jit(solution)/shard_map/ppermute | solution.py:201
  4.5 47.6 %collective-permute-start.7 = (bf16[256,2048]{1,0:T(8,128)(2,1)}, bf16[256,2048]{1,0:T(8,128)(2,1)}, u32[]{:S(2)}, u32[]{:S(2)}) collective-permute-start(bf16[256,2048]{1,0:T(8,128)(2,1)} %bitcast.23), channel_id=1, source_target_pairs={{0,30},{2,28},{4,26},{6,24},{24,6},{26,4},{28,2},{30,0},{1,31},{3,... | collective-permute-start | bytes 3145736 | tf_op jit(solution)/shard_map/ppermute | solution.py:201
  9.6 48.3 %collective-permute-start.4 = (bf16[256,2048]{1,0:T(8,128)(2,1)}, bf16[256,2048]{1,0:T(8,128)(2,1)}, u32[]{:S(2)}, u32[]{:S(2)}) collective-permute-start(bf16[256,2048]{1,0:T(8,128)(2,1)} %bitcast.24), channel_id=1, source_target_pairs={{2,0},{4,2},{6,4},{8,6},{10,8},{12,10},{14,12},{16,14},{18,16},{20... | collective-permute-start | bytes 3145736 | tf_op jit(solution)/shard_map/ppermute | solution.py:201
  49.4 2.7 %copy-start.10 = (bf16[256,2048]{1,0:T(8,128)(2,1)}, bf16[256,2048]{1,0:T(8,128)(2,1)S(1)}, u32[]{:S(2)}) copy-start(bf16[256,2048]{1,0:T(8,128)(2,1)S(1)} %collective-permute-done) | copy-start | bytes 3145732
  49.4 8.6 %copy-start.9 = (bf16[256,2048]{1,0:T(8,128)(2,1)S(1)}, bf16[256,2048]{1,0:T(8,128)(2,1)}, u32[]{:S(2)}) copy-start(bf16[256,2048]{1,0:T(8,128)(2,1)} %param.11) | copy-start | bytes 3145732
  49.5 37.2 %collective-permute-start.1 = (bf16[256,2048]{1,0:T(8,128)(2,1)S(1)}, bf16[256,2048]{1,0:T(8,128)(2,1)S(1)}, u32[]{:S(2)}, u32[]{:S(2)}) collective-permute-start(bf16[256,2048]{1,0:T(8,128)(2,1)S(1)} %broadcast_select_fusion.2.refs_0_), channel_id=1, source_target_pairs={{0,1},{1,0},{2,3},{3,2},{4,5},{5,4},{6,7},{7,6},{8,9},{9,8},{10,11... | collective-permute-start | bytes 3145736 | tf_op jit(solution)/shard_map/ppermute | solution.py:22
  52.1 7.8 %copy-start.7 = (bf16[1,2048]{1,0:T(2,128)(2,1)S(1)}, bf16[1,2048]{1,0:T(2,128)(2,1)}, u32[]{:S(2)}) copy-start(bf16[1,2048]{1,0:T(2,128)(2,1)} %refs_4_.1) | copy-start | bytes 12292
  52.1 36.2 %copy-start = (bf16[1,4096,512]{2,1,0:T(8,128)(2,1)S(1)}, bf16[1,4096,512]{2,1,0:T(8,128)(2,1)}, u32[]{:S(2)}) copy-start(bf16[1,4096,512]{2,1,0:T(8,128)(2,1)} %param.15) | copy-start | bytes 12582916
  53.6 34.7 %copy-start.1 = (bf16[1,4096,256]{2,1,0:T(8,128)(2,1)S(1)}, bf16[1,4096,256]{2,1,0:T(8,128)(2,1)}, u32[]{:S(2)}) copy-start(bf16[1,4096,256]{2,1,0:T(8,128)(2,1)} %param.16) | copy-start | bytes 6291460
  53.6 43.6 %collective-permute-start.8 = (bf16[256,2048]{1,0:T(8,128)(2,1)S(1)}, bf16[256,2048]{1,0:T(8,128)(2,1)S(1)}, u32[]{:S(2)}, u32[]{:S(2)}) collective-permute-start(bf16[256,2048]{1,0:T(8,128)(2,1)S(1)} %broadcast_select_fusion.refs_0_.refs_2_), channel_id=1, source_target_pairs={{0,1},{1,0},{2,3},{3,2},{4,5},{5,4},{6,7},{7,6},{8,9},{9,8},{10,11... | collective-permute-start | bytes 3145736 | tf_op jit(solution)/shard_map/ppermute | solution.py:22
  59.3 41.5 %collective-permute-start.5 = (bf16[256,2048]{1,0:T(8,128)(2,1)S(1)}, bf16[256,2048]{1,0:T(8,128)(2,1)S(1)}, u32[]{:S(2)}, u32[]{:S(2)}) collective-permute-start(bf16[256,2048]{1,0:T(8,128)(2,1)S(1)} %broadcast_select_fusion.1.refs_0_), channel_id=1, source_target_pairs={{0,1},{1,0},{2,3},{3,2},{4,5},{5,4},{6,7},{7,6},{8,9},{9,8},{10,11... | collective-permute-start | bytes 3145736 | tf_op jit(solution)/shard_map/ppermute | solution.py:22
  59.9 2.3 %collective-permute-start.2 = (bf16[1,2048]{1,0:T(2,128)(2,1)S(1)}, bf16[1,2048]{1,0:T(2,128)(2,1)S(1)}, u32[]{:S(2)}, u32[]{:S(2)}) collective-permute-start(bf16[1,2048]{1,0:T(2,128)(2,1)S(1)} %copy-done.7), channel_id=1, source_target_pairs={{0,1},{1,0},{2,3},{3,2},{4,5},{5,4},{6,7},{7,6},{8,9},{9,8},{10,11... | collective-permute-start | bytes 12296 | tf_op jit(solution)/shard_map/ppermute | solution.py:22
  59.9 68.7 %collective-permute-start.10 = (bf16[256,2048]{1,0:T(8,128)(2,1)}, bf16[256,2048]{1,0:T(8,128)(2,1)}, u32[]{:S(2)}, u32[]{:S(2)}) collective-permute-start(bf16[256,2048]{1,0:T(8,128)(2,1)} %bitcast), channel_id=1, source_target_pairs={{8,20},{10,18},{12,16},{14,14},{16,12},{18,10},{20,8},{22,6},{9,21... | collective-permute-start | bytes 3145736 | tf_op jit(solution)/shard_map/ppermute | solution.py:201
  62.2 67.5 %collective-permute-start.11 = (bf16[256,2048]{1,0:T(8,128)(2,1)}, bf16[256,2048]{1,0:T(8,128)(2,1)}, u32[]{:S(2)}, u32[]{:S(2)}) collective-permute-start(bf16[256,2048]{1,0:T(8,128)(2,1)} %bitcast), channel_id=1, source_target_pairs={{0,28},{2,26},{4,24},{6,22},{1,29},{3,27},{5,25},{7,23}} | collective-permute-start | bytes 3145736 | tf_op jit(solution)/shard_map/ppermute | solution.py:201
  86.7 43.0 %collective-permute-start.9 = (bf16[256,2048]{1,0:T(8,128)(2,1)}, bf16[256,2048]{1,0:T(8,128)(2,1)}, u32[]{:S(2)}, u32[]{:S(2)}) collective-permute-start(bf16[256,2048]{1,0:T(8,128)(2,1)} %copy-done.10), channel_id=1, source_target_pairs={{26,4},{28,2},{30,0},{27,5},{29,3},{31,1}} | collective-permute-start | bytes 3145736 | tf_op jit(solution)/shard_map/ppermute | solution.py:201
  88.3 2.2 %copy-start.2 = (bf16[1,512,4096]{2,1,0:T(8,128)(2,1)S(1)}, bf16[1,512,4096]{2,1,0:T(8,128)(2,1)}, u32[]{:S(2)}) copy-start(bf16[1,512,4096]{2,1,0:T(8,128)(2,1)} %param.17) | copy-start | bytes 12582916
  97.3 35.4 %collective-permute-start.3 = (bf16[256,2048]{1,0:T(8,128)(2,1)}, bf16[256,2048]{1,0:T(8,128)(2,1)}, u32[]{:S(2)}, u32[]{:S(2)}) collective-permute-start(bf16[256,2048]{1,0:T(8,128)(2,1)} %get-tuple-element.15), channel_id=1, source_target_pairs={{0,1},{1,0},{2,3},{3,2},{4,5},{5,4},{6,7},{7,6},{8,9},{9,8},{10,11... | collective-permute-start | bytes 3145736 | tf_op jit(solution)/shard_map/ppermute | solution.py:22
  105.6 1.0 copy-start.5
  106.6 1.0 copy-start.8
  107.6 24.9 %collective-permute-start.13 = (f32[256,128]{1,0:T(8,128)S(1)}, f32[256,128]{1,0:T(8,128)S(1)}, u32[]{:S(2)}, u32[]{:S(2)}) collective-permute-start(f32[256,128]{1,0:T(8,128)S(1)} %get-tuple-element.19), channel_id=1, source_target_pairs={{0,1},{1,0},{2,3},{3,2},{4,5},{5,4},{6,7},{7,6},{8,9},{9,8},{10,11... | collective-permute-start | bytes 393224 | tf_op jit(solution)/shard_map/ppermute | solution.py:22
  128.7 4.0 %copy-start.4 = (bf16[256,2048]{1,0:T(8,128)(2,1)S(1)}, bf16[256,2048]{1,0:T(8,128)(2,1)}, u32[]{:S(2)}) copy-start(bf16[256,2048]{1,0:T(8,128)(2,1)} %copy-done.3) | copy-start | bytes 3145732
  128.7 6.8 %collective-permute-start.12 = (bf16[256,2048]{1,0:T(8,128)(2,1)}, bf16[256,2048]{1,0:T(8,128)(2,1)S(1)}, u32[]{:S(2)}, u32[]{:S(2)}) collective-permute-start(bf16[256,2048]{1,0:T(8,128)(2,1)} %copy-done.8), channel_id=1, source_target_pairs={{0,1},{1,0},{2,3},{3,2},{4,5},{5,4},{6,7},{7,6},{8,9},{9,8},{10,11... | collective-permute-start | bytes 3145736 | tf_op jit(solution)/shard_map/ppermute | solution.py:22
  132.7 2.8 %copy-start.6 = (bf16[256,2048]{1,0:T(8,128)(2,1)S(1)}, bf16[256,2048]{1,0:T(8,128)(2,1)}, u32[]{:S(2)}) copy-start(bf16[256,2048]{1,0:T(8,128)(2,1)} %copy-done.5) | copy-start | bytes 3145732
  (1 other events, 1.0 us)

commit v2 on v1

--- a/solution.py
+++ b/solution.py
@@ -195,38 +195,25 @@
 
     block = sections // 4
     high = sections - block
-    near, far = range(block, high), [*range(block), *range(high, sections)]
 
     def send(value, pairs):
         return lax.ppermute(value, "section", pairs)
 
-    fetched_near = send(stash_held, [(s, sections - 1 - s) for s in near])
-    arrived = send(held, [(s, s + 1) for s in range(sections - 1)])
-    coming = send(grads_held, [(s + 1, s) for s in range(sections - 1)])
-    evicted_near = send(held, [(s, sections - 2 - s) for s in near])
-    fetched_far = send(stash_held, [(s, sections - 1 - s) for s in far])
+    up = [(s, s + 1) for s in range(sections - 1)]
+    crossing = send(held, [(s, t) for s, t in up if t % block == 0])
+    fetched = send(stash_held, [(s, sections - 1 - s) for s in range(sections)])
+    coming = send(grads_held, [(t, s) for s, t in up])
+    inside = send(held, [(s, t) for s, t in up if t % block])
+    evicted_near = send(held, [(s, sections - 2 - s) for s in range(block, high)])
     evicted_far = send(held, [(s, sections - 2 - s) for s in range(block)])
-    relayed = send(arrived, [(s, sections - 1 - s) for s in range(high + 1, sections)])
-    fetched = jnp.where((position >= block) & (position < high), fetched_near, fetched_far)
-
+    relayed = send(inside, [(s, sections - 1 - s) for s in range(high + 1, sections)])
     gains = gathered(norm_gain, "tensor")
 
-    x_shard = jnp.where(position == 0, embedded, arrived)
-    xs = gathered(x_shard, "tensor")
     normed = pltpu.VMEM((seq, model), BF16)
     shares = [shape((seq, width), BF16)] * count
     proj = 2 * seq * model * (qcols + kvcols)
     out_flops = 2 * seq * model * qcols
     moved = 2 * model * (2 * qcols + kvcols)
-    parts = call(
-        forward_kernel, count, heads,
-        [*xs, *gains, wq, wkv, wo], shares,
-        [normed, pltpu.VMEM((seq, qcols), BF16)],
-        proj + out_flops, moved,
-    )
-    mixed = reduced(parts, "tensor")
-    section_out = (x_shard.astype(F32) + mixed).astype(BF16)
-
     bs = gathered(fetched, "tensor")
     query, keyval, prob, inv = call(
         recompute_kernel, count, heads,
@@ -240,6 +227,19 @@
         [normed],
         proj, moved,
     )
+    position, _ = lax.optimization_barrier((position, inv))
+    arrived = jnp.where(position % block == 0, crossing, inside)
+    x_shard = jnp.where(position == 0, embedded, arrived)
+    xs = gathered(x_shard, "tensor")
+    parts = call(
+        forward_kernel, count, heads,
+        [*xs, *gains, wq, wkv, wo], shares,
+        [normed, pltpu.VMEM((seq, qcols), BF16)],
+        proj + out_flops, moved,
+    )
+    mixed = reduced(parts, "tensor")
+    section_out = (x_shard.astype(F32) + mixed).astype(BF16)
+
     g_shard = jnp.where(position == sections - 1, loss_grad, coming)
     gs = gathered(g_shard, "tensor")
     *terms, total = call(
@@ -249,7 +249,14 @@
         [pltpu.VMEM((seq, qcols), BF16)],
         proj + out_flops, moved,
     )
-    place, last, _ = lax.optimization_barrier((position, embedded, total))
+    d_normed = reduced(terms, "tensor")
+    total = sum(gathered(total, "tensor"))[:, :1]
+    inv = inv[:, :1]
+    scaled = d_normed * norm_gain.astype(F32)
+    result = (
+        g_shard.astype(F32) + inv * scaled - fetched.astype(F32) * inv**3 * (total / model)
+    ).astype(BF16)
+    place, last, _ = lax.optimization_barrier((position, embedded, (result, section_out)))
     evicted = jnp.where(
         place < block - 1,
         relayed,
@@ -257,14 +264,7 @@
             place < high - 1, evicted_near, jnp.where(place < sections - 1, evicted_far, last)
         ),
     )
-    d_normed = reduced(terms, "tensor")
-    total = sum(gathered(total, "tensor"))[:, :1]
-    inv = inv[:, :1]
-    scaled = d_normed * norm_gain.astype(F32)
-    result = (
-        g_shard.astype(F32) + inv * scaled - fetched.astype(F32) * inv**3 * (total / model)
-    )
-    return section_out[None], evicted[None], result.astype(BF16)[None]
+    return section_out[None], evicted[None], result[None]
 
 
 def solution(mesh):

time: 138 us -> 163 us (1.18)
  starting transfers between devices: 45.3 us -> 62.1 us
  local copies, waits for them, and re-layouts: 5.18 us -> 10.9 us
  waiting for transfers between devices: 62.1 us -> 67.4 us
  other arithmetic: 10.6 us -> 7.6 us
    ppermute x7, starting transfers between devices: 39.5 us -> 56.5 us  [send(): return lax.ppermute(value, 'section', pairs)]
    broadcast_in_dim x3 -> x1, other arithmetic: 7.39 us -> 1.16 us  [local(): return (section_out[None], evicted[None], result[None])]
    unnamed x22 -> x36, local copies, waits for them, and re-layouts: 5.18 us -> 10.9 us
    ppermute x7, waiting for transfers between devices: 61.1 us -> 66.3 us  [send(): return lax.ppermute(value, 'section', pairs)]
    convert_element_type x0 -> x2, other arithmetic: none -> 3.33 us  [the longest x1 1.83 us: local(): result = (g_shard.astype(F32) + inv * scaled - fetched.astype(F32) * inv...]
  transfers between devices with their start and end apart: 14 -> 14, of which waited for: 4 -> 5; matrix products, arithmetic and copies ran while one was open for 6% -> 4% of each run, Pallas kernels for 10% -> 9%
where the time goes in v2:
time: 163 us
  waiting for transfers between devices  67.4 us (41%)
  starting transfers between devices  62.1 us (38%)
  Pallas kernels  14.1 us (9%)
  local copies, waits for them, and re-layouts  10.9 us (7%)
  other arithmetic  7.6 us (5%)
    ppermute x7, waiting for transfers between devices, send(): return lax.ppermute(value, 'section', pairs)  66.3 us
    ppermute x7, starting transfers between devices, send(): return lax.ppermute(value, 'section', pairs)  56.5 us
    pallas_call x3, Pallas kernels, call(): pl.pallas_call(functools.partial(kernel, count, heads), out_shape=out_sha...  14.1 us
    unnamed x36, local copies, waits for them, and re-layouts  10.9 us
    ppermute x7, starting transfers between devices, rotate(): lax.ppermute(value, axis, [(i, (i - k) % count) for i in range(count)])  5.59 us
  transfers between devices with their start and end apart: 14, of which 5 were waited for; matrix products, arithmetic and copies ran while one was open for 4% of the time, Pallas kernels for 9%

profile of v2, /device:TPU:7, one launch (start us, length us, event | category | flops | bytes accessed | tf_op | source)
XLA Modules:
  0.0 162.9 jit_solution(10301826970936811838)
XLA Ops:
  0.6 3.3 %collective-permute-start = (bf16[256,2048]{1,0:T(8,128)(2,1)}, bf16[256,2048]{1,0:T(8,128)(2,1)S(1)}, u32[]{:S(2)}, u32[]{:S(2)}) collective-permute-start(bf16[256,2048]{1,0:T(8,128)(2,1)} %bitcast.22), channel_id=1, source_target_pairs={{0,30},{2,28},{4,26},{6,24},{8,22},{10,20},{12,18},{14,16},{16,14}... | collective-permute-start | bytes 3145736 | tf_op jit(solution)/shard_map/ppermute | solution.py:200
  3.9 24.7 %collective-permute-done.refs_0_.refs_2_ = bf16[256,2048]{1,0:T(8,128)(2,1)S(1)} collective-permute-done((bf16[256,2048]{1,0:T(8,128)(2,1)}, bf16[256,2048]{1,0:T(8,128)(2,1)S(1)}, u32[]{:S(2)}, u32[]{:S(2)}) %collective-permute-start) | collective-permute-done | bytes 1048608 | tf_op jit(solution)/shard_map/ppermute | solution.py:200
  28.6 1.5 collective-permute-start.1
  30.2 1.3 collective-permute-start.4
  31.5 27.5 %collective-permute-start.3 = (bf16[256,2048]{1,0:T(8,128)(2,1)}, bf16[256,2048]{1,0:T(8,128)(2,1)}, u32[]{:S(2)}, u32[]{:S(2)}) collective-permute-start(bf16[256,2048]{1,0:T(8,128)(2,1)} %bitcast.3), channel_id=1, source_target_pairs={{6,8},{14,16},{22,24},{7,9},{15,17},{23,25}} | collective-permute-start | bytes 3145736 | tf_op jit(solution)/shard_map/ppermute | solution.py:200
  59.0 1.9 %collective-permute-start.7 = (bf16[256,2048]{1,0:T(8,128)(2,1)}, bf16[256,2048]{1,0:T(8,128)(2,1)}, u32[]{:S(2)}, u32[]{:S(2)}) collective-permute-start(bf16[256,2048]{1,0:T(8,128)(2,1)} %bitcast.23), channel_id=1, source_target_pairs={{2,0},{4,2},{6,4},{8,6},{10,8},{12,10},{14,12},{16,14},{18,16},{20... | collective-permute-start | bytes 3145736 | tf_op jit(solution)/shard_map/ppermute | solution.py:200
  62.6 2.6 %copy-done = bf16[1,4096,512]{2,1,0:T(8,128)(2,1)S(1)} copy-done((bf16[1,4096,512]{2,1,0:T(8,128)(2,1)S(1)}, bf16[1,4096,512]{2,1,0:T(8,128)(2,1)}, u32[]{:S(2)}) %copy-start) | copy-done | bytes 4194328
  65.1 1.6 copy-done.3
  67.4 2.8 %shard_map.112 = (bf16[256,512]{1,0:T(8,128)(2,1)S(1)}, bf16[256,256]{1,0:T(8,128)(2,1)S(1)}, f32[4,256,256]{2,1,0:T(8,128)S(1)}, f32[256,128]{1,0:T(8,128)S(1)}) custom-call(bf16[256,2048]{1,0:T(8,128)(2,1)S(1)} %collective-permute-done.refs_0_.refs_2_, bf16[256,2048]{1,0:T(8,128)(2,1)S(1)} %collective-permute-done.1.refs_1_.refs_3_, ...), custom_call_target="tpu_custom_call" | custom-call | flops 1610612736 | bytes 10485760 | tf_op jit(solution)/shard_map/pallas_call | solution.py:171
  71.8 8.7 %collective-permute-done.3 = bf16[256,2048]{1,0:T(8,128)(2,1)} collective-permute-done((bf16[256,2048]{1,0:T(8,128)(2,1)}, bf16[256,2048]{1,0:T(8,128)(2,1)}, u32[]{:S(2)}, u32[]{:S(2)}) %collective-permute-start.3) | collective-permute-done | bytes 1048608 | tf_op jit(solution)/shard_map/ppermute | solution.py:200
  80.6 1.5 select_select_fusion.refs_0_
  83.3 3.8 %collective-permute-done.7 = bf16[256,2048]{1,0:T(8,128)(2,1)} collective-permute-done((bf16[256,2048]{1,0:T(8,128)(2,1)}, bf16[256,2048]{1,0:T(8,128)(2,1)}, u32[]{:S(2)}, u32[]{:S(2)}) %collective-permute-start.7) | collective-permute-done | bytes 1048608 | tf_op jit(solution)/shard_map/ppermute | solution.py:200
  87.1 1.3 broadcast_select_fusion.refs_0_
  88.5 1.5 collective-permute-start.8
  90.0 2.2 %copy-done.1 = bf16[1,4096,512]{2,1,0:T(8,128)(2,1)S(1)} copy-done((bf16[1,4096,512]{2,1,0:T(8,128)(2,1)S(1)}, bf16[1,4096,512]{2,1,0:T(8,128)(2,1)}, u32[]{:S(2)}) %copy-start.1) | copy-done | bytes 4194328
  92.2 2.2 %copy-done.5 = bf16[1,512,4096]{2,1,0:T(8,128)(2,1)S(1)} copy-done((bf16[1,512,4096]{2,1,0:T(8,128)(2,1)S(1)}, bf16[1,512,4096]{2,1,0:T(8,128)(2,1)}, u32[]{:S(2)}) %copy-start.5) | copy-done | bytes 4194328
  94.4 6.7 %shard_map.113 = (bf16[256,2048]{1,0:T(8,128)(2,1)S(1)}, bf16[256,2048]{1,0:T(8,128)(2,1)S(1)}) custom-call(bf16[256,2048]{1,0:T(8,128)(2,1)S(1)} %select_select_fusion.refs_0_, bf16[256,2048]{1,0:T(8,128)(2,1)} %collective-permute-done.5.refs_1_, bf16[1,2048]{1,0:T(2,128)(2,1)S(1)} %copy-done.15, ...), custom_call_target="tpu_custom_call" | custom-call | flops 2684354560 | bytes 10485760 | tf_op jit(solution)/shard_map/pallas_call | solution.py:171
  101.2 4.6 %shard_map.114 = (bf16[256,2048]{1,0:T(8,128)(2,1)S(1)}, bf16[256,2048]{1,0:T(8,128)(2,1)S(1)}, f32[256,128]{1,0:T(8,128)S(1)}) custom-call(bf16[256,2048]{1,0:T(8,128)(2,1)S(1)} %broadcast_select_fusion.refs_0_, bf16[256,2048]{1,0:T(8,128)(2,1)S(1)} %collective-permute-done.8.refs_1_, bf16[256,2048]{1,0:T(8,128)(2,1)S(1)} %copy-done.7, ...), custom_call_target="tpu_custom_call" | custom-call | flops 2684354560 | bytes 10485760 | tf_op jit(solution)/shard_map/pallas_call | solution.py:171
  106.5 1.3 collective-permute-start.12
  107.8 19.6 %collective-permute-start.13 = (bf16[256,2048]{1,0:T(8,128)(2,1)}, bf16[256,2048]{1,0:T(8,128)(2,1)S(1)}, u32[]{:S(2)}, u32[]{:S(2)}) collective-permute-start(bf16[256,2048]{1,0:T(8,128)(2,1)} %bitcast.3), channel_id=1, source_target_pairs={{0,28},{2,26},{4,24},{6,22},{1,29},{3,27},{5,25},{7,23}} | collective-permute-start | bytes 3145736 | tf_op jit(solution)/shard_map/ppermute | solution.py:200
  127.6 1.6 collective-permute-start.11
  129.4 1.5 add_convert_fusion
  130.9 1.8 %subtract_convert_fusion = bf16[256,2048]{1,0:T(8,128)(2,1)} fusion(bf16[256,2048]{1,0:T(8,128)(2,1)S(1)} %copy-done.7, bf16[256,2048]{1,0:T(8,128)(2,1)S(1)} %collective-permute-done.9, bf16[256,2048]{1,0:T(8,128)(2,1)S(1)} %get-tuple-element.22, bf16[256,2048]{1,0:T(8,128)(2,1)S(1)} %broadcast_select_fusion.refs_0_, f32[256]{0:T(256)S(1)} %fusion.2, ...), kind=kLoop, calls=%fused_computation | loop fusion | flops 6291456 | bytes 5254144 | tf_op jit(solution)/shard_map/convert_element_type | solution.py:258
  132.7 29.0 %collective-permute-done.12 = bf16[256,2048]{1,0:T(8,128)(2,1)S(1)} collective-permute-done((bf16[256,2048]{1,0:T(8,128)(2,1)}, bf16[256,2048]{1,0:T(8,128)(2,1)S(1)}, u32[]{:S(2)}, u32[]{:S(2)}) %collective-permute-start.12) | collective-permute-done | bytes 1048608 | tf_op jit(solution)/shard_map/ppermute | solution.py:200
  (51 shorter events, 7.4 us)
Async XLA Ops:
  0.6 28.0 %collective-permute-start = (bf16[256,2048]{1,0:T(8,128)(2,1)}, bf16[256,2048]{1,0:T(8,128)(2,1)S(1)}, u32[]{:S(2)}, u32[]{:S(2)}) collective-permute-start(bf16[256,2048]{1,0:T(8,128)(2,1)} %bitcast.22), channel_id=1, source_target_pairs={{0,30},{2,28},{4,26},{6,24},{8,22},{10,20},{12,18},{14,16},{16,14}... | collective-permute-start | bytes 3145736 | tf_op jit(solution)/shard_map/ppermute | solution.py:200
  28.6 41.6 %copy-start.6 = (bf16[256,2048]{1,0:T(8,128)(2,1)}, bf16[256,2048]{1,0:T(8,128)(2,1)S(1)}, u32[]{:S(2)}) copy-start(bf16[256,2048]{1,0:T(8,128)(2,1)S(1)} %collective-permute-done.refs_0_.refs_2_) | copy-start | bytes 3145732
  28.6 33.9 %collective-permute-start.1 = (bf16[256,2048]{1,0:T(8,128)(2,1)S(1)}, bf16[256,2048]{1,0:T(8,128)(2,1)S(1)}, u32[]{:S(2)}, u32[]{:S(2)}) collective-permute-start(bf16[256,2048]{1,0:T(8,128)(2,1)S(1)} %collective-permute-done.refs_0_.refs_2_), channel_id=1, source_target_pairs={{0,1},{1,0},{2,3},{3,2},{4,5},{5,4},{6,7},{7,6},{8,9},{9,8},{10,11... | collective-permute-start | bytes 3145736 | tf_op jit(solution)/shard_map/ppermute | solution.py:22
  30.2 41.7 %collective-permute-start.4 = (bf16[256,2048]{1,0:T(8,128)(2,1)}, bf16[256,2048]{1,0:T(8,128)(2,1)}, u32[]{:S(2)}, u32[]{:S(2)}) collective-permute-start(bf16[256,2048]{1,0:T(8,128)(2,1)} %bitcast.3), channel_id=1, source_target_pairs={{0,2},{2,4},{4,6},{8,10},{10,12},{12,14},{16,18},{18,20},{20,22},{... | collective-permute-start | bytes 3145736 | tf_op jit(solution)/shard_map/ppermute | solution.py:200
  31.5 49.1 %collective-permute-start.3 = (bf16[256,2048]{1,0:T(8,128)(2,1)}, bf16[256,2048]{1,0:T(8,128)(2,1)}, u32[]{:S(2)}, u32[]{:S(2)}) collective-permute-start(bf16[256,2048]{1,0:T(8,128)(2,1)} %bitcast.3), channel_id=1, source_target_pairs={{6,8},{14,16},{22,24},{7,9},{15,17},{23,25}} | collective-permute-start | bytes 3145736 | tf_op jit(solution)/shard_map/ppermute | solution.py:200
  59.0 28.1 %collective-permute-start.7 = (bf16[256,2048]{1,0:T(8,128)(2,1)}, bf16[256,2048]{1,0:T(8,128)(2,1)}, u32[]{:S(2)}, u32[]{:S(2)}) collective-permute-start(bf16[256,2048]{1,0:T(8,128)(2,1)} %bitcast.23), channel_id=1, source_target_pairs={{2,0},{4,2},{6,4},{8,6},{10,8},{12,10},{14,12},{16,14},{18,16},{20... | collective-permute-start | bytes 3145736 | tf_op jit(solution)/shard_map/ppermute | solution.py:200
  60.9 1.7 %collective-permute-start.2 = (bf16[1,2048]{1,0:T(2,128)(2,1)}, bf16[1,2048]{1,0:T(2,128)(2,1)S(1)}, u32[]{:S(2)}, u32[]{:S(2)}) collective-permute-start(bf16[1,2048]{1,0:T(2,128)(2,1)} %refs_4_.1), channel_id=1, source_target_pairs={{0,1},{1,0},{2,3},{3,2},{4,5},{5,4},{6,7},{7,6},{8,9},{9,8},{10,11... | collective-permute-start | bytes 12296 | tf_op jit(solution)/shard_map/ppermute | solution.py:22
  62.6 7.6 %copy-start.8 = (bf16[256,2048]{1,0:T(8,128)(2,1)}, bf16[256,2048]{1,0:T(8,128)(2,1)S(1)}, u32[]{:S(2)}) copy-start(bf16[256,2048]{1,0:T(8,128)(2,1)S(1)} %collective-permute-done.1.refs_1_.refs_3_) | copy-start | bytes 3145732
  67.4 13.1 %copy-start.16 = (bf16[256,2048]{1,0:T(8,128)(2,1)S(1)}, bf16[256,2048]{1,0:T(8,128)(2,1)}, u32[]{:S(2)}) copy-start(bf16[256,2048]{1,0:T(8,128)(2,1)} %param.9) | copy-start | bytes 3145732
  82.1 7.9 %copy-start.4 = (bf16[1,4096,256]{2,1,0:T(8,128)(2,1)S(1)}, bf16[1,4096,256]{2,1,0:T(8,128)(2,1)}, u32[]{:S(2)}) copy-start(bf16[1,4096,256]{2,1,0:T(8,128)(2,1)} %param.16) | copy-start | bytes 6291460
  82.1 7.9 %copy-start.15 = (bf16[1,2048]{1,0:T(2,128)(2,1)S(1)}, bf16[1,2048]{1,0:T(2,128)(2,1)}, u32[]{:S(2)}) copy-start(bf16[1,2048]{1,0:T(2,128)(2,1)} %refs_4_.1) | copy-start | bytes 12292
  82.1 7.9 %collective-permute-start.5 = (bf16[256,2048]{1,0:T(8,128)(2,1)S(1)}, bf16[256,2048]{1,0:T(8,128)(2,1)}, u32[]{:S(2)}, u32[]{:S(2)}) collective-permute-start(bf16[256,2048]{1,0:T(8,128)(2,1)S(1)} %select_select_fusion.refs_0_), channel_id=1, source_target_pairs={{0,1},{1,0},{2,3},{3,2},{4,5},{5,4},{6,7},{7,6},{8,9},{9,8},{10,11... | collective-permute-start | bytes 3145736 | tf_op jit(solution)/shard_map/ppermute | solution.py:22
  88.5 12.7 %collective-permute-start.8 = (bf16[256,2048]{1,0:T(8,128)(2,1)S(1)}, bf16[256,2048]{1,0:T(8,128)(2,1)S(1)}, u32[]{:S(2)}, u32[]{:S(2)}) collective-permute-start(bf16[256,2048]{1,0:T(8,128)(2,1)S(1)} %broadcast_select_fusion.refs_0_), channel_id=1, source_target_pairs={{0,1},{1,0},{2,3},{3,2},{4,5},{5,4},{6,7},{7,6},{8,9},{9,8},{10,11... | collective-permute-start | bytes 3145736 | tf_op jit(solution)/shard_map/ppermute | solution.py:22
  94.4 6.9 %copy-start.7 = (bf16[256,2048]{1,0:T(8,128)(2,1)S(1)}, bf16[256,2048]{1,0:T(8,128)(2,1)}, u32[]{:S(2)}) copy-start(bf16[256,2048]{1,0:T(8,128)(2,1)} %copy-done.6) | copy-start | bytes 3145732
  94.4 6.9 %copy-start.9 = (bf16[256,2048]{1,0:T(8,128)(2,1)S(1)}, bf16[256,2048]{1,0:T(8,128)(2,1)}, u32[]{:S(2)}) copy-start(bf16[256,2048]{1,0:T(8,128)(2,1)} %copy-done.8) | copy-start | bytes 3145732
  94.4 6.9 %copy-start.11 = (f32[4,256,256]{2,1,0:T(8,128)S(1)}, f32[4,256,256]{2,1,0:T(8,128)}, u32[]{:S(2)}) copy-start(f32[4,256,256]{2,1,0:T(8,128)} %copy-done.10) | copy-start | bytes 3145732
  101.1 28.2 %collective-permute-start.6 = (bf16[256,2048]{1,0:T(8,128)(2,1)S(1)}, bf16[256,2048]{1,0:T(8,128)(2,1)S(1)}, u32[]{:S(2)}, u32[]{:S(2)}) collective-permute-start(bf16[256,2048]{1,0:T(8,128)(2,1)S(1)} %get-tuple-element.18), channel_id=1, source_target_pairs={{0,1},{1,0},{2,3},{3,2},{4,5},{5,4},{6,7},{7,6},{8,9},{9,8},{10,11... | collective-permute-start | bytes 3145736 | tf_op jit(solution)/shard_map/ppermute | solution.py:22
  101.2 26.2 %copy-start.13 = (f32[256,128]{1,0:T(8,128)S(1)}, f32[256,128]{1,0:T(8,128)}, u32[]{:S(2)}) copy-start(f32[256,128]{1,0:T(8,128)} %copy-done.12) | copy-start | bytes 393220
  105.9 25.0 %collective-permute-start.9 = (bf16[256,2048]{1,0:T(8,128)(2,1)S(1)}, bf16[256,2048]{1,0:T(8,128)(2,1)S(1)}, u32[]{:S(2)}, u32[]{:S(2)}) collective-permute-start(bf16[256,2048]{1,0:T(8,128)(2,1)S(1)} %get-tuple-element.23), channel_id=1, source_target_pairs={{0,1},{1,0},{2,3},{3,2},{4,5},{5,4},{6,7},{7,6},{8,9},{9,8},{10,11... | collective-permute-start | bytes 3145736 | tf_op jit(solution)/shard_map/ppermute | solution.py:22
  106.4 21.2 %collective-permute-start.10 = (f32[256,128]{1,0:T(8,128)S(1)}, f32[256,128]{1,0:T(8,128)S(1)}, u32[]{:S(2)}, u32[]{:S(2)}) collective-permute-start(f32[256,128]{1,0:T(8,128)S(1)} %get-tuple-element.24), channel_id=1, source_target_pairs={{0,1},{1,0},{2,3},{3,2},{4,5},{5,4},{6,7},{7,6},{8,9},{9,8},{10,11... | collective-permute-start | bytes 393224 | tf_op jit(solution)/shard_map/ppermute | solution.py:22
  106.5 55.2 %collective-permute-start.12 = (bf16[256,2048]{1,0:T(8,128)(2,1)}, bf16[256,2048]{1,0:T(8,128)(2,1)S(1)}, u32[]{:S(2)}, u32[]{:S(2)}) collective-permute-start(bf16[256,2048]{1,0:T(8,128)(2,1)} %bitcast.3), channel_id=1, source_target_pairs={{8,20},{10,18},{12,16},{14,14},{16,12},{18,10},{20,8},{22,6},{9,21... | collective-permute-start | bytes 3145736 | tf_op jit(solution)/shard_map/ppermute | solution.py:200
  107.8 54.0 %collective-permute-start.13 = (bf16[256,2048]{1,0:T(8,128)(2,1)}, bf16[256,2048]{1,0:T(8,128)(2,1)S(1)}, u32[]{:S(2)}, u32[]{:S(2)}) collective-permute-start(bf16[256,2048]{1,0:T(8,128)(2,1)} %bitcast.3), channel_id=1, source_target_pairs={{0,28},{2,26},{4,24},{6,22},{1,29},{3,27},{5,25},{7,23}} | collective-permute-start | bytes 3145736 | tf_op jit(solution)/shard_map/ppermute | solution.py:200
  127.6 34.1 %collective-permute-start.11 = (bf16[256,2048]{1,0:T(8,128)(2,1)}, bf16[256,2048]{1,0:T(8,128)(2,1)}, u32[]{:S(2)}, u32[]{:S(2)}) collective-permute-start(bf16[256,2048]{1,0:T(8,128)(2,1)} %collective-permute-done.4), channel_id=1, source_target_pairs={{26,4},{28,2},{30,0},{27,5},{29,3},{31,1}} | collective-permute-start | bytes 3145736 | tf_op jit(solution)/shard_map/ppermute | solution.py:200
  130.9 30.9 %copy-start.17 = (bf16[256,2048]{1,0:T(8,128)(2,1)S(1)}, bf16[256,2048]{1,0:T(8,128)(2,1)}, u32[]{:S(2)}) copy-start(bf16[256,2048]{1,0:T(8,128)(2,1)} %param.9) | copy-start | bytes 3145732
  (8 other events, 17.7 us)
